TPU v7x, 32 devices: a whole 2x2x4 slice. The times are simulated.
32 devices in a mesh: dp: 2 (over x), ctx: 16 (over z, y, core).
Axes of the slice: x: 2, y: 2, z: 4, core: 2. Of those that a mesh axis runs over, the one named last changes fastest.
Arguments:
- features: bfloat16 [2, 2048, 1536], P('dp', 'ctx'), may hold values from -500 to 500
- gain: float32 [1536], replicated, may hold values from 0.1 to 1.9
- conv_weight: bfloat16 [5, 1536, 768], replicated, may hold values from -0.0625 to 0.0625
- cotangent: bfloat16 [2, 2048, 768], P('dp', 'ctx'), may hold values from -15 to 15
Outputs:
- convolved: bfloat16 [2, 2048, 768], P('dp', 'ctx')
- input_grad: bfloat16 [2, 2048, 1536], P('dp', 'ctx')
- gain_grad: float32 [1536], replicated
All inputs are finite; a program needn't handle non-finite values.
Results may differ from a plain program's by a relative error of at most 0.0054.
Values may be sent and summed in bfloat16 or wider, within the bound.
A program may use at most 64 MiB of HBM per device.

v0:
```python
import math
import jax
import jax.numpy as jnp
from jax import lax
from jax.sharding import PartitionSpec as P

KERNEL_TAPS = 5
EPS = 1e-06


def shifted(block, axis, distance):
    devices = range(lax.axis_size(axis))
    route = [(i - distance, i) for i in devices if i - distance in devices]
    return lax.ppermute(block, axis, route)


def activate(values):
    return jax.nn.gelu(values, approximate=True)


def flip_channels(values):
    return values[:, :, ::-1]


def taps_ahead(values, shard_hops):
    pieces = []
    for tap_index in range(KERNEL_TAPS):
        if tap_index == KERNEL_TAPS // 2:
            pieces.append(values)
        else:
            pieces.append(shifted(values, "ctx", -(tap_index - KERNEL_TAPS // 2) * shard_hops))
    return pieces


def taps_behind(values, shard_hops):
    pieces = []
    for tap_index in range(KERNEL_TAPS):
        if tap_index == KERNEL_TAPS // 2:
            pieces.append(values)
        else:
            pieces.append(shifted(values, "ctx", (tap_index - KERNEL_TAPS // 2) * shard_hops))
    return pieces


def apply_forward(pieces, weight):
    lead = pieces[0].shape[0]
    middle = pieces[0].shape[1]
    total = jnp.zeros((lead * middle, weight.shape[2]), jnp.float32)
    for tap_index in range(KERNEL_TAPS):
        flat_rows = pieces[tap_index].reshape(lead * middle, pieces[tap_index].shape[2])
        total = total + jnp.dot(flat_rows, weight[tap_index], preferred_element_type=jnp.float32)
    return total.reshape(lead, middle, weight.shape[2])


def apply_backward(pieces, weight):
    lead = pieces[0].shape[0]
    middle = pieces[0].shape[1]
    total = jnp.zeros((lead * middle, weight.shape[1]), jnp.float32)
    for tap_index in range(KERNEL_TAPS):
        flat_rows = pieces[tap_index].reshape(lead * middle, pieces[tap_index].shape[2])
        total = total + lax.dot_general(
            flat_rows,
            weight[tap_index],
            (((1,), (1,)), ((), ())),
            preferred_element_type=jnp.float32,
        )
    return total.reshape(lead, middle, weight.shape[1])


def per_device(features, gain, conv_weight, cotangent):
    shard_hops = lax.axis_size("ctx") // 8
    wide = features.astype(jnp.float32)
    inv_rms = lax.rsqrt(jnp.mean(wide * wide, axis=-1, keepdims=True) + EPS)
    normed = wide * inv_rms
    scaled = normed * gain
    hidden = activate(scaled).astype(jnp.bfloat16)
    ahead = taps_ahead(hidden, shard_hops)
    forward_term = apply_forward(ahead, conv_weight)
    flipped = [
        flip_channels(ahead[KERNEL_TAPS - 1 - tap_index]) for tap_index in range(KERNEL_TAPS)
    ]
    reverse_term = flip_channels(apply_forward(flipped, conv_weight).astype(jnp.bfloat16))
    convolved = (forward_term + reverse_term.astype(jnp.float32)).astype(jnp.bfloat16)
    behind = taps_behind(cotangent, shard_hops)
    back_forward = apply_backward(behind, conv_weight)
    flipped_grads = [
        flip_channels(behind[KERNEL_TAPS - 1 - tap_index]) for tap_index in range(KERNEL_TAPS)
    ]
    back_reverse = flip_channels(apply_backward(flipped_grads, conv_weight).astype(jnp.bfloat16))
    grad_hidden = back_forward + back_reverse.astype(jnp.float32)
    _, pullback = jax.vjp(activate, scaled)
    grad_scaled = pullback(grad_hidden)[0]
    partial_sum = jnp.sum(grad_scaled * normed, axis=(0, 1))
    summed = lax.psum(partial_sum, ("dp", "ctx"))
    total_rows = features.shape[0] * features.shape[1] * lax.axis_size("dp") * lax.axis_size("ctx")
    gain_grad = summed / math.sqrt(total_rows)
    grad_normed = grad_scaled * gain
    spread_term = jnp.mean(grad_normed * normed, axis=-1, keepdims=True)
    input_grad = (inv_rms * (grad_normed - normed * spread_term)).astype(jnp.bfloat16)
    return (convolved, input_grad, gain_grad)


def solution(mesh):
    return jax.shard_map(
        per_device,
        mesh=mesh,
        in_specs=(P("dp", "ctx", None), P(), P(), P("dp", "ctx", None)),
        out_specs=(P("dp", "ctx", None), P("dp", "ctx", None), P()),
        check_vma=False,
    )
```

profile of v0, /device:TPU:0, one launch (start us, length us, event | category | flops | bytes accessed | tf_op | source)
XLA Modules:
  0.0 152.5 jit_solution(12865565920787407074)
XLA Ops:
  0.6 4.9 %collective-permute-start.6 = (bf16[1,128,768]{2,1,0:T(8,128)(2,1)}, bf16[1,128,768]{2,1,0:T(8,128)(2,1)S(1)}, u32[]{:S(2)}, u32[]{:S(2)}) collective-permute-start(bf16[1,128,768]{2,1,0:T(8,128)(2,1)} %param.7), channel_id=1, source_target_pairs={{0,2},{1,3},{2,4},{3,5},{4,6},{5,7},{6,8},{7,9},{8,10},{9,11},{10,... | collective-permute-start | bytes 589832 | tf_op jit(solution)/shard_map/ppermute | solution.py:14
  5.5 3.5 %collective-permute-start.7 = (bf16[1,128,768]{2,1,0:T(8,128)(2,1)}, bf16[1,128,768]{2,1,0:T(8,128)(2,1)S(1)}, u32[]{:S(2)}, u32[]{:S(2)}) collective-permute-start(bf16[1,128,768]{2,1,0:T(8,128)(2,1)} %param.7), channel_id=1, source_target_pairs={{0,4},{1,5},{2,6},{3,7},{4,8},{5,9},{6,10},{7,11},{8,12},{9,13},{1... | collective-permute-start | bytes 589832 | tf_op jit(solution)/shard_map/ppermute | solution.py:14
  9.0 1.3 collective-permute-start.4
  10.3 1.3 collective-permute-start.5
  11.6 2.7 %rev.39 = bf16[1,128,768]{2,1,0:T(8,128)(2,1)S(1)} reverse(bf16[1,128,768]{2,1,0:T(8,128)(2,1)} %param.7), dimensions={2} | reverse | bytes 393216 | tf_op jit(solution)/shard_map/rev | solution.py:22
  14.3 2.7 %fusion.23 = f32[128,1536]{1,0:T(8,128)S(1)} fusion(bf16[5,1536,768]{2,1,0:T(8,128)(2,1)} %param.6, bf16[1,128,768]{2,1,0:T(8,128)(2,1)} %param.7), kind=kOutput, calls=%fused_computation.27 | convolution fusion | flops 301989888 | bytes 3342336 | tf_op jit(solution)/shard_map/dot_general | solution.py:61
  17.0 2.6 %fusion.21 = f32[128,1536]{1,0:T(8,128)S(1)} fusion(bf16[5,1536,768]{2,1,0:T(8,128)(2,1)} %param.6, bf16[1,128,768]{2,1,0:T(8,128)(2,1)S(1)} %rev.39), kind=kOutput, calls=%fused_computation.25 | convolution fusion | flops 301989888 | bytes 3342336 | tf_op jit(solution)/shard_map/dot_general | solution.py:61
  19.5 1.2 fusion.116
  20.7 0.0 collective-permute-done.6
  20.7 0.6 rev.38
  21.4 2.5 %fusion.29 = f32[128,1536]{1,0:T(8,128)S(1)} fusion(bf16[5,1536,768]{2,1,0:T(8,128)(2,1)} %param.6, bf16[1,128,768]{2,1,0:T(8,128)(2,1)S(1)} %rev.38), kind=kOutput, calls=%fused_computation.33 | convolution fusion | flops 301989888 | bytes 3342336 | tf_op jit(solution)/shard_map/dot_general | solution.py:61
  23.9 0.0 copy-start.1
  24.0 0.7 copy-done.1
  24.6 2.2 %rev.37 = bf16[1,128,768]{2,1,0:T(8,128)(2,1)} reverse(bf16[1,128,768]{2,1,0:T(8,128)(2,1)S(1)} %collective-permute-done.7), dimensions={2} | reverse | bytes 393216 | tf_op jit(solution)/shard_map/rev | solution.py:22
  26.8 2.7 %fusion.1 = f32[128,1536]{1,0:T(8,128)S(1)} fusion(f32[128,1536]{1,0:T(8,128)S(1)} %fusion.21, f32[128,1536]{1,0:T(8,128)S(1)} %fusion.29, bf16[5,1536,768]{2,1,0:T(8,128)(2,1)} %param.6, bf16[1,128,768]{2,1,0:T(8,128)(2,1)} %rev.37), kind=kOutput, calls=%fused_computation.3 | convolution fusion | flops 302383104 | bytes 4915200 | tf_op jit(solution)/shard_map/dot_general | solution.py:61
  29.6 0.0 copy-start.2
  29.6 2.7 %rev.41 = bf16[1,128,768]{2,1,0:T(8,128)(2,1)S(1)} reverse(bf16[1,128,768]{2,1,0:T(8,128)(2,1)} %collective-permute-done.4), dimensions={2} | reverse | bytes 393216 | tf_op jit(solution)/shard_map/rev | solution.py:22
  32.3 2.6 %fusion.7 = f32[128,1536]{1,0:T(8,128)S(1)} fusion(bf16[5,1536,768]{2,1,0:T(8,128)(2,1)} %param.6, bf16[1,128,768]{2,1,0:T(8,128)(2,1)S(1)} %rev.41), kind=kOutput, calls=%fused_computation.11 | convolution fusion | flops 301989888 | bytes 3342336 | tf_op jit(solution)/shard_map/dot_general | solution.py:61
  34.9 2.7 %rev.40 = bf16[1,128,768]{2,1,0:T(8,128)(2,1)S(1)} reverse(bf16[1,128,768]{2,1,0:T(8,128)(2,1)} %collective-permute-done.5), dimensions={2} | reverse | bytes 393216 | tf_op jit(solution)/shard_map/rev | solution.py:22
  37.5 2.6 %fusion.6 = bf16[128,1536]{1,0:T(8,128)(2,1)S(1)} fusion(f32[128,1536]{1,0:T(8,128)S(1)} %fusion.7, f32[128,1536]{1,0:T(8,128)S(1)} %fusion.1, bf16[5,1536,768]{2,1,0:T(8,128)(2,1)} %param.6, bf16[1,128,768]{2,1,0:T(8,128)(2,1)S(1)} %rev.40), kind=kOutput, calls=%fused_computation.10 | convolution fusion | flops 302579712 | bytes 4521984 | tf_op jit(solution)/shard_map/dot_general | solution.py:61
  40.1 1.2 reverse.7
  41.3 2.7 %fusion.31 = f32[128,1536]{1,0:T(8,128)S(1)} fusion(bf16[5,1536,768]{2,1,0:T(8,128)(2,1)} %param.6, bf16[1,128,768]{2,1,0:T(8,128)(2,1)} %collective-permute-done.5), kind=kOutput, calls=%fused_computation.35 | convolution fusion | flops 301989888 | bytes 3342336 | tf_op jit(solution)/shard_map/dot_general | solution.py:61
  44.0 2.5 %fusion.9 = f32[128,1536]{1,0:T(8,128)S(1)} fusion(bf16[5,1536,768]{2,1,0:T(8,128)(2,1)} %param.6, bf16[1,128,768]{2,1,0:T(8,128)(2,1)S(1)} %copy-done.2), kind=kOutput, calls=%fused_computation.13 | convolution fusion | flops 301989888 | bytes 3342336 | tf_op jit(solution)/shard_map/dot_general | solution.py:61
  46.5 2.7 %fusion.4 = f32[128,1536]{1,0:T(8,128)S(1)} fusion(f32[128,1536]{1,0:T(8,128)S(1)} %fusion.23, f32[128,1536]{1,0:T(8,128)S(1)} %fusion.31, bf16[5,1536,768]{2,1,0:T(8,128)(2,1)} %param.6, bf16[1,128,768]{2,1,0:T(8,128)(2,1)} %collective-permute-done.4), kind=kOutput, calls=%fused_computation.8 | convolution fusion | flops 302383104 | bytes 4915200 | tf_op jit(solution)/shard_map/dot_general | solution.py:61
  49.3 3.1 %fusion.115 = (f32[1536]{0:T(1024)S(1)}, f32[128]{0:T(128)S(1)}, f32[1,128,1536]{2,1,0:T(8,128)S(1)}) fusion(bf16[1,128,1536]{2,1,0:T(8,128)(2,1)S(1)} %copy-done, f32[128]{0:T(128)S(1)} %add_rsqrt_fusion, f32[1536]{0:T(1024)S(1)} %copy-done.5, bf16[128,1536]{1,0:T(8,128)(2,1)S(1)} %reverse.7, f32[128,1536]{1,0:T(8,128)S(1)} %fusion.9, ...), kind=kOutput, calls=%fused_computation.99 | convolution fusion | flops 308083072 | bytes 5714944 | tf_op jit(solution)/shard_map/dot_general | solution.py:61
  52.4 1.3 fusion.114
  53.7 5.5 %collective-permute-start = (bf16[1,128,1536]{2,1,0:T(8,128)(2,1)S(1)}, bf16[1,128,1536]{2,1,0:T(8,128)(2,1)S(1)}, u32[]{:S(2)}, u32[]{:S(2)}) collective-permute-start(bf16[1,128,1536]{2,1,0:T(8,128)(2,1)S(1)} %get-tuple-element.6), channel_id=1, source_target_pairs={{0,4},{1,5},{2,6},{3,7},{4,8},{5,9},{6,10},{7,11},{8,12},{9,13},{1... | collective-permute-start | bytes 1179656 | tf_op jit(solution)/shard_map/ppermute | solution.py:14
  59.2 3.6 %collective-permute-start.1 = (bf16[1,128,1536]{2,1,0:T(8,128)(2,1)S(1)}, bf16[1,128,1536]{2,1,0:T(8,128)(2,1)S(1)}, u32[]{:S(2)}, u32[]{:S(2)}) collective-permute-start(bf16[1,128,1536]{2,1,0:T(8,128)(2,1)S(1)} %get-tuple-element.6), channel_id=1, source_target_pairs={{0,2},{1,3},{2,4},{3,5},{4,6},{5,7},{6,8},{7,9},{8,10},{9,11},{10,... | collective-permute-start | bytes 1179656 | tf_op jit(solution)/shard_map/ppermute | solution.py:14
  62.8 1.3 collective-permute-start.2
  64.1 1.3 collective-permute-start.3
  65.4 1.2 rev.34
  66.6 2.1 %fusion.27 = f32[128,768]{1,0:T(8,128)S(1)} fusion(bf16[5,1536,768]{2,1,0:T(8,128)(2,1)} %param.6, bf16[1,128,1536]{2,1,0:T(8,128)(2,1)S(1)} %get-tuple-element.6), kind=kOutput, calls=%fused_computation.31 | convolution fusion | flops 301989888 | bytes 3145728 | tf_op jit(solution)/shard_map/dot_general | solution.py:51
  68.8 47.5 %psum.7 = f32[1536]{0:T(1024)S(1)} all-reduce(f32[1536]{0:T(1024)S(1)} %get-tuple-element.3), channel_id=1, replica_groups=mesh['dp'=2,'ctx'=16] {'dp','ctx'}, use_global_device_ids=true, to_apply=%region_3.0 | all-reduce | flops 1536 | bytes 12288 | tf_op jit(solution)/shard_map/psum | solution.py:94
  116.3 2.1 %fusion.25 = f32[128,768]{1,0:T(8,128)S(1)} fusion(bf16[5,1536,768]{2,1,0:T(8,128)(2,1)} %param.6, bf16[1,128,1536]{2,1,0:T(8,128)(2,1)S(1)} %rev.34), kind=kOutput, calls=%fused_computation.29 | convolution fusion | flops 301989888 | bytes 3145728 | tf_op jit(solution)/shard_map/dot_general | solution.py:51
  118.5 0.6 broadcast_multiply_fusion
  119.1 1.2 rev.36
  120.3 2.1 %fusion.11 = f32[128,768]{1,0:T(8,128)S(1)} fusion(bf16[5,1536,768]{2,1,0:T(8,128)(2,1)} %param.6, bf16[1,128,1536]{2,1,0:T(8,128)(2,1)S(1)} %rev.36), kind=kOutput, calls=%fused_computation.15 | convolution fusion | flops 301989888 | bytes 3145728 | tf_op jit(solution)/shard_map/dot_general | solution.py:51
  122.5 1.2 rev.35
  123.7 2.1 %fusion.17 = f32[128,768]{1,0:T(8,128)S(1)} fusion(bf16[5,1536,768]{2,1,0:T(8,128)(2,1)} %param.6, bf16[1,128,1536]{2,1,0:T(8,128)(2,1)S(1)} %rev.35), kind=kOutput, calls=%fused_computation.21 | convolution fusion | flops 301989888 | bytes 3145728 | tf_op jit(solution)/shard_map/dot_general | solution.py:51
  125.9 6.7 %rev.33 = bf16[1,128,1536]{2,1,0:T(8,128)(2,1)} reverse(bf16[1,128,1536]{2,1,0:T(8,128)(2,1)} %collective-permute-done.2), dimensions={2} | reverse | bytes 786432 | tf_op jit(solution)/shard_map/rev | solution.py:22
  132.6 2.3 %fusion.33 = f32[128,768]{1,0:T(8,128)S(1)} fusion(bf16[5,1536,768]{2,1,0:T(8,128)(2,1)} %param.6, bf16[1,128,1536]{2,1,0:T(8,128)(2,1)} %rev.33), kind=kOutput, calls=%fused_computation.37 | convolution fusion | flops 301989888 | bytes 3145728 | tf_op jit(solution)/shard_map/dot_general | solution.py:51
  134.9 5.2 %rev.32 = bf16[1,128,1536]{2,1,0:T(8,128)(2,1)S(1)} reverse(bf16[1,128,1536]{2,1,0:T(8,128)(2,1)} %collective-permute-done.3), dimensions={2} | reverse | bytes 786432 | tf_op jit(solution)/shard_map/rev | solution.py:22
  140.1 2.2 %fusion.90 = bf16[128,768]{1,0:T(8,128)(2,1)S(1)} fusion(f32[128,768]{1,0:T(8,128)S(1)} %fusion.11, f32[128,768]{1,0:T(8,128)S(1)} %fusion.17, f32[128,768]{1,0:T(8,128)S(1)} %fusion.25, f32[128,768]{1,0:T(8,128)S(1)} %fusion.33, bf16[5,1536,768]{2,1,0:T(8,128)(2,1)} %param.6, bf16[1,128,1536]{2,1,0:T(8,128)(2,1)S(1)} %rev.32), kind=kOutput, calls=%fused_computation.76 | convolution fusion | flops 302481408 | bytes 4521984 | tf_op jit(solution)/shard_map/dot_general | solution.py:51
  142.2 0.6 reverse.6
  142.9 2.3 %fusion.13 = f32[128,768]{1,0:T(8,128)S(1)} fusion(bf16[5,1536,768]{2,1,0:T(8,128)(2,1)} %param.6, bf16[1,128,1536]{2,1,0:T(8,128)(2,1)} %collective-permute-done.3), kind=kOutput, calls=%fused_computation.17 | convolution fusion | flops 301989888 | bytes 3145728 | tf_op jit(solution)/shard_map/dot_general | solution.py:51
  145.2 2.3 %fusion.19 = f32[128,768]{1,0:T(8,128)S(1)} fusion(bf16[5,1536,768]{2,1,0:T(8,128)(2,1)} %param.6, bf16[1,128,1536]{2,1,0:T(8,128)(2,1)} %collective-permute-done.2), kind=kOutput, calls=%fused_computation.23 | convolution fusion | flops 301989888 | bytes 3145728 | tf_op jit(solution)/shard_map/dot_general | solution.py:51
  147.5 2.1 %fusion.35 = f32[128,768]{1,0:T(8,128)S(1)} fusion(bf16[5,1536,768]{2,1,0:T(8,128)(2,1)} %param.6, bf16[1,128,1536]{2,1,0:T(8,128)(2,1)S(1)} %collective-permute-done.1), kind=kOutput, calls=%fused_computation.39 | convolution fusion | flops 301989888 | bytes 3145728 | tf_op jit(solution)/shard_map/dot_general | solution.py:51
  149.6 2.9 %fusion.96 = bf16[1,128,768]{2,1,0:T(8,128)(2,1)} fusion(f32[128,768]{1,0:T(8,128)S(1)} %fusion.13, f32[128,768]{1,0:T(8,128)S(1)} %fusion.19, f32[128,768]{1,0:T(8,128)S(1)} %fusion.27, f32[128,768]{1,0:T(8,128)S(1)} %fusion.35, bf16[5,1536,768]{2,1,0:T(8,128)(2,1)} %param.6, bf16[1,128,1536]{2,1,0:T(8,128)(2,1)S(1)} %collective-permute-done, ...), kind=kOutput, calls=%fused_computation.78 | convolution fusion | flops 302678016 | bytes 4718592 | tf_op jit(solution)/shard_map/dot_general | solution.py:51
  (18 shorter events, 0.1 us)
Async XLA Ops:
  0.6 20.1 %collective-permute-start.6 = (bf16[1,128,768]{2,1,0:T(8,128)(2,1)}, bf16[1,128,768]{2,1,0:T(8,128)(2,1)S(1)}, u32[]{:S(2)}, u32[]{:S(2)}) collective-permute-start(bf16[1,128,768]{2,1,0:T(8,128)(2,1)} %param.7), channel_id=1, source_target_pairs={{0,2},{1,3},{2,4},{3,5},{4,6},{5,7},{6,8},{7,9},{8,10},{9,11},{10,... | collective-permute-start | bytes 589832 | tf_op jit(solution)/shard_map/ppermute | solution.py:14
  5.5 18.4 %collective-permute-start.7 = (bf16[1,128,768]{2,1,0:T(8,128)(2,1)}, bf16[1,128,768]{2,1,0:T(8,128)(2,1)S(1)}, u32[]{:S(2)}, u32[]{:S(2)}) collective-permute-start(bf16[1,128,768]{2,1,0:T(8,128)(2,1)} %param.7), channel_id=1, source_target_pairs={{0,4},{1,5},{2,6},{3,7},{4,8},{5,9},{6,10},{7,11},{8,12},{9,13},{1... | collective-permute-start | bytes 589832 | tf_op jit(solution)/shard_map/ppermute | solution.py:14
  9.0 20.5 %collective-permute-start.4 = (bf16[1,128,768]{2,1,0:T(8,128)(2,1)}, bf16[1,128,768]{2,1,0:T(8,128)(2,1)}, u32[]{:S(2)}, u32[]{:S(2)}) collective-permute-start(bf16[1,128,768]{2,1,0:T(8,128)(2,1)} %param.7), channel_id=1, source_target_pairs={{4,0},{5,1},{6,2},{7,3},{8,4},{9,5},{10,6},{11,7},{12,8},{13,9},{1... | collective-permute-start | bytes 589832 | tf_op jit(solution)/shard_map/ppermute | solution.py:14
  10.3 24.5 %collective-permute-start.5 = (bf16[1,128,768]{2,1,0:T(8,128)(2,1)}, bf16[1,128,768]{2,1,0:T(8,128)(2,1)}, u32[]{:S(2)}, u32[]{:S(2)}) collective-permute-start(bf16[1,128,768]{2,1,0:T(8,128)(2,1)} %param.7), channel_id=1, source_target_pairs={{2,0},{3,1},{4,2},{5,3},{6,4},{7,5},{8,6},{9,7},{10,8},{11,9},{12,... | collective-permute-start | bytes 589832 | tf_op jit(solution)/shard_map/ppermute | solution.py:14
  20.7 3.2 %copy-start.3 = (bf16[1,128,768]{2,1,0:T(8,128)(2,1)}, bf16[1,128,768]{2,1,0:T(8,128)(2,1)S(1)}, u32[]{:S(2)}) copy-start(bf16[1,128,768]{2,1,0:T(8,128)(2,1)S(1)} %collective-permute-done.6) | copy-start | bytes 589828
  23.9 0.7 copy-start.1
  26.8 22.4 %copy-start = (bf16[1,128,1536]{2,1,0:T(8,128)(2,1)S(1)}, bf16[1,128,1536]{2,1,0:T(8,128)(2,1)}, u32[]{:S(2)}) copy-start(bf16[1,128,1536]{2,1,0:T(8,128)(2,1)} %param.4) | copy-start | bytes 1179652
  26.8 22.4 %copy-start.5 = (f32[1536]{0:T(1024)S(1)}, f32[1536]{0:T(1024)}, u32[]{:S(2)}) copy-start(f32[1536]{0:T(1024)} %param.5) | copy-start | bytes 18436
  29.6 14.4 %copy-start.2 = (bf16[1,128,768]{2,1,0:T(8,128)(2,1)S(1)}, bf16[1,128,768]{2,1,0:T(8,128)(2,1)}, u32[]{:S(2)}) copy-start(bf16[1,128,768]{2,1,0:T(8,128)(2,1)} %copy-done.1) | copy-start | bytes 589828
  40.1 9.2 %copy-start.4 = (bf16[1,128,768]{2,1,0:T(8,128)(2,1)S(1)}, bf16[1,128,768]{2,1,0:T(8,128)(2,1)}, u32[]{:S(2)}) copy-start(bf16[1,128,768]{2,1,0:T(8,128)(2,1)} %copy-done.3) | copy-start | bytes 589828
  53.7 65.4 %collective-permute-start = (bf16[1,128,1536]{2,1,0:T(8,128)(2,1)S(1)}, bf16[1,128,1536]{2,1,0:T(8,128)(2,1)S(1)}, u32[]{:S(2)}, u32[]{:S(2)}) collective-permute-start(bf16[1,128,1536]{2,1,0:T(8,128)(2,1)S(1)} %get-tuple-element.6), channel_id=1, source_target_pairs={{0,4},{1,5},{2,6},{3,7},{4,8},{5,9},{6,10},{7,11},{8,12},{9,13},{1... | collective-permute-start | bytes 1179656 | tf_op jit(solution)/shard_map/ppermute | solution.py:14
  59.2 63.3 %collective-permute-start.1 = (bf16[1,128,1536]{2,1,0:T(8,128)(2,1)S(1)}, bf16[1,128,1536]{2,1,0:T(8,128)(2,1)S(1)}, u32[]{:S(2)}, u32[]{:S(2)}) collective-permute-start(bf16[1,128,1536]{2,1,0:T(8,128)(2,1)S(1)} %get-tuple-element.6), channel_id=1, source_target_pairs={{0,2},{1,3},{2,4},{3,5},{4,6},{5,7},{6,8},{7,9},{8,10},{9,11},{10,... | collective-permute-start | bytes 1179656 | tf_op jit(solution)/shard_map/ppermute | solution.py:14
  62.8 63.0 %collective-permute-start.2 = (bf16[1,128,1536]{2,1,0:T(8,128)(2,1)S(1)}, bf16[1,128,1536]{2,1,0:T(8,128)(2,1)}, u32[]{:S(2)}, u32[]{:S(2)}) collective-permute-start(bf16[1,128,1536]{2,1,0:T(8,128)(2,1)S(1)} %get-tuple-element.6), channel_id=1, source_target_pairs={{2,0},{3,1},{4,2},{5,3},{6,4},{7,5},{8,6},{9,7},{10,8},{11,9},{12,... | collective-permute-start | bytes 1179656 | tf_op jit(solution)/shard_map/ppermute | solution.py:14
  64.1 70.7 %collective-permute-start.3 = (bf16[1,128,1536]{2,1,0:T(8,128)(2,1)S(1)}, bf16[1,128,1536]{2,1,0:T(8,128)(2,1)}, u32[]{:S(2)}, u32[]{:S(2)}) collective-permute-start(bf16[1,128,1536]{2,1,0:T(8,128)(2,1)S(1)} %get-tuple-element.6), channel_id=1, source_target_pairs={{4,0},{5,1},{6,2},{7,3},{8,4},{9,5},{10,6},{11,7},{12,8},{13,9},{1... | collective-permute-start | bytes 1179656 | tf_op jit(solution)/shard_map/ppermute | solution.py:14
where the time goes:
time: 155 us; the launch traced here: 153 us
  matrix products  49.2 us (32%)
  blocking collectives  47.5 us (31%)
  local copies, waits for them, and re-layouts  28.9 us (19%)
  starting transfers between devices  22.7 us (15%)
  other arithmetic  3.03 us (2%)
    psum x1, blocking collectives, per_device(): summed = lax.psum(partial_sum, ('dp', 'ctx'))  47.5 us
    dot_general x10, matrix products, apply_backward(): lax.dot_general(flat_rows, weight[tap_index], (((1,), (1,)), ((), ())), p...  26.6 us
    rev x10, local copies, waits for them, and re-layouts, flip_channels(): return values[:, :, ::-1]  26.4 us
    ppermute x8, starting transfers between devices, shifted(): return lax.ppermute(block, axis, route)  22.7 us
    dot_general x10, matrix products, apply_forward(): jnp.dot(flat_rows, weight[tap_index], preferred_element_type=jnp.float32)  22.6 us
  transfers between devices with their start and end apart: 8, of which 0 were waited for; matrix products, arithmetic and copies ran while one was open for 29% of the time, Pallas kernels for 0%

commit v1 on v0

--- a/solution.py
+++ b/solution.py
@@ -91,7 +91,9 @@
     _, pullback = jax.vjp(activate, scaled)
     grad_scaled = pullback(grad_hidden)[0]
     partial_sum = jnp.sum(grad_scaled * normed, axis=(0, 1))
-    summed = lax.psum(partial_sum, ("dp", "ctx"))
+    summed = partial_sum
+    for mesh_axis in ("dp", "ctx"):
+        summed = lax.psum(summed, mesh_axis)
     total_rows = features.shape[0] * features.shape[1] * lax.axis_size("dp") * lax.axis_size("ctx")
     gain_grad = summed / math.sqrt(total_rows)
     grad_normed = grad_scaled * gain

time: 155 us -> 147 us (0.948)
  blocking collectives: 47.5 us -> 39.7 us
    psum x1 -> x2, blocking collectives: 47.5 us -> 39.7 us  [per_device(): summed = lax.psum(summed, mesh_axis)]
  transfers between devices with their start and end apart: 8 -> 8, of which waited for: 0 -> 0; matrix products, arithmetic and copies ran while one was open for 29% -> 31% of each run, Pallas kernels for 0% -> 0%
where the time goes in v1:
time: 147 us; the launch traced here: 145 us
  matrix products  49.2 us (33%)
  blocking collectives  39.7 us (27%)
  local copies, waits for them, and re-layouts  28.9 us (20%)
  starting transfers between devices  22.7 us (15%)
  other arithmetic  3.03 us (2%)
    psum x2, blocking collectives, per_device(): summed = lax.psum(summed, mesh_axis)  39.7 us
    dot_general x10, matrix products, apply_backward(): lax.dot_general(flat_rows, weight[tap_index], (((1,), (1,)), ((), ())), p...  26.6 us
    rev x10, local copies, waits for them, and re-layouts, flip_channels(): return values[:, :, ::-1]  26.4 us
    ppermute x8, starting transfers between devices, shifted(): return lax.ppermute(block, axis, route)  22.7 us
    dot_general x10, matrix products, apply_forward(): jnp.dot(flat_rows, weight[tap_index], preferred_element_type=jnp.float32)  22.6 us
  transfers between devices with their start and end apart: 8, of which 0 were waited for; matrix products, arithmetic and copies ran while one was open for 31% of the time, Pallas kernels for 0%

profile of v1, /device:TPU:0, one launch (start us, length us, event | category | flops | bytes accessed | tf_op | source)
XLA Modules:
  0.0 144.7 jit_solution(13048756174272062120)
XLA Ops:
  0.6 4.9 %collective-permute-start.6 = (bf16[1,128,768]{2,1,0:T(8,128)(2,1)}, bf16[1,128,768]{2,1,0:T(8,128)(2,1)S(1)}, u32[]{:S(2)}, u32[]{:S(2)}) collective-permute-start(bf16[1,128,768]{2,1,0:T(8,128)(2,1)} %param.7), channel_id=1, source_target_pairs={{0,2},{1,3},{2,4},{3,5},{4,6},{5,7},{6,8},{7,9},{8,10},{9,11},{10,... | collective-permute-start | bytes 589832 | tf_op jit(solution)/shard_map/ppermute | solution.py:14
  5.5 3.5 %collective-permute-start.7 = (bf16[1,128,768]{2,1,0:T(8,128)(2,1)}, bf16[1,128,768]{2,1,0:T(8,128)(2,1)S(1)}, u32[]{:S(2)}, u32[]{:S(2)}) collective-permute-start(bf16[1,128,768]{2,1,0:T(8,128)(2,1)} %param.7), channel_id=1, source_target_pairs={{0,4},{1,5},{2,6},{3,7},{4,8},{5,9},{6,10},{7,11},{8,12},{9,13},{1... | collective-permute-start | bytes 589832 | tf_op jit(solution)/shard_map/ppermute | solution.py:14
  9.0 1.3 collective-permute-start.4
  10.3 1.3 collective-permute-start.5
  11.6 2.7 %rev.39 = bf16[1,128,768]{2,1,0:T(8,128)(2,1)S(1)} reverse(bf16[1,128,768]{2,1,0:T(8,128)(2,1)} %param.7), dimensions={2} | reverse | bytes 393216 | tf_op jit(solution)/shard_map/rev | solution.py:22
  14.3 2.7 %fusion.23 = f32[128,1536]{1,0:T(8,128)S(1)} fusion(bf16[5,1536,768]{2,1,0:T(8,128)(2,1)} %param.6, bf16[1,128,768]{2,1,0:T(8,128)(2,1)} %param.7), kind=kOutput, calls=%fused_computation.27 | convolution fusion | flops 301989888 | bytes 3342336 | tf_op jit(solution)/shard_map/dot_general | solution.py:61
  17.0 2.6 %fusion.21 = f32[128,1536]{1,0:T(8,128)S(1)} fusion(bf16[5,1536,768]{2,1,0:T(8,128)(2,1)} %param.6, bf16[1,128,768]{2,1,0:T(8,128)(2,1)S(1)} %rev.39), kind=kOutput, calls=%fused_computation.25 | convolution fusion | flops 301989888 | bytes 3342336 | tf_op jit(solution)/shard_map/dot_general | solution.py:61
  19.5 1.2 fusion.116
  20.7 0.6 rev.38
  21.4 2.5 %fusion.29 = f32[128,1536]{1,0:T(8,128)S(1)} fusion(bf16[5,1536,768]{2,1,0:T(8,128)(2,1)} %param.6, bf16[1,128,768]{2,1,0:T(8,128)(2,1)S(1)} %rev.38), kind=kOutput, calls=%fused_computation.33 | convolution fusion | flops 301989888 | bytes 3342336 | tf_op jit(solution)/shard_map/dot_general | solution.py:61
  23.9 0.0 copy-start.1
  24.0 0.7 copy-done.1
  24.6 2.2 %rev.37 = bf16[1,128,768]{2,1,0:T(8,128)(2,1)} reverse(bf16[1,128,768]{2,1,0:T(8,128)(2,1)S(1)} %collective-permute-done.7), dimensions={2} | reverse | bytes 393216 | tf_op jit(solution)/shard_map/rev | solution.py:22
  26.8 2.7 %fusion.1 = f32[128,1536]{1,0:T(8,128)S(1)} fusion(f32[128,1536]{1,0:T(8,128)S(1)} %fusion.21, f32[128,1536]{1,0:T(8,128)S(1)} %fusion.29, bf16[5,1536,768]{2,1,0:T(8,128)(2,1)} %param.6, bf16[1,128,768]{2,1,0:T(8,128)(2,1)} %rev.37), kind=kOutput, calls=%fused_computation.3 | convolution fusion | flops 302383104 | bytes 4915200 | tf_op jit(solution)/shard_map/dot_general | solution.py:61
  29.6 0.0 copy-start.2
  29.6 2.7 %rev.41 = bf16[1,128,768]{2,1,0:T(8,128)(2,1)S(1)} reverse(bf16[1,128,768]{2,1,0:T(8,128)(2,1)} %collective-permute-done.4), dimensions={2} | reverse | bytes 393216 | tf_op jit(solution)/shard_map/rev | solution.py:22
  32.3 2.6 %fusion.7 = f32[128,1536]{1,0:T(8,128)S(1)} fusion(bf16[5,1536,768]{2,1,0:T(8,128)(2,1)} %param.6, bf16[1,128,768]{2,1,0:T(8,128)(2,1)S(1)} %rev.41), kind=kOutput, calls=%fused_computation.11 | convolution fusion | flops 301989888 | bytes 3342336 | tf_op jit(solution)/shard_map/dot_general | solution.py:61
  34.9 2.7 %rev.40 = bf16[1,128,768]{2,1,0:T(8,128)(2,1)S(1)} reverse(bf16[1,128,768]{2,1,0:T(8,128)(2,1)} %collective-permute-done.5), dimensions={2} | reverse | bytes 393216 | tf_op jit(solution)/shard_map/rev | solution.py:22
  37.5 2.6 %fusion.6 = bf16[128,1536]{1,0:T(8,128)(2,1)S(1)} fusion(f32[128,1536]{1,0:T(8,128)S(1)} %fusion.7, f32[128,1536]{1,0:T(8,128)S(1)} %fusion.1, bf16[5,1536,768]{2,1,0:T(8,128)(2,1)} %param.6, bf16[1,128,768]{2,1,0:T(8,128)(2,1)S(1)} %rev.40), kind=kOutput, calls=%fused_computation.10 | convolution fusion | flops 302579712 | bytes 4521984 | tf_op jit(solution)/shard_map/dot_general | solution.py:61
  40.1 1.2 reverse.7
  41.3 2.7 %fusion.31 = f32[128,1536]{1,0:T(8,128)S(1)} fusion(bf16[5,1536,768]{2,1,0:T(8,128)(2,1)} %param.6, bf16[1,128,768]{2,1,0:T(8,128)(2,1)} %collective-permute-done.5), kind=kOutput, calls=%fused_computation.35 | convolution fusion | flops 301989888 | bytes 3342336 | tf_op jit(solution)/shard_map/dot_general | solution.py:61
  44.0 2.5 %fusion.9 = f32[128,1536]{1,0:T(8,128)S(1)} fusion(bf16[5,1536,768]{2,1,0:T(8,128)(2,1)} %param.6, bf16[1,128,768]{2,1,0:T(8,128)(2,1)S(1)} %copy-done.2), kind=kOutput, calls=%fused_computation.13 | convolution fusion | flops 301989888 | bytes 3342336 | tf_op jit(solution)/shard_map/dot_general | solution.py:61
  46.5 2.7 %fusion.4 = f32[128,1536]{1,0:T(8,128)S(1)} fusion(f32[128,1536]{1,0:T(8,128)S(1)} %fusion.23, f32[128,1536]{1,0:T(8,128)S(1)} %fusion.31, bf16[5,1536,768]{2,1,0:T(8,128)(2,1)} %param.6, bf16[1,128,768]{2,1,0:T(8,128)(2,1)} %collective-permute-done.4), kind=kOutput, calls=%fused_computation.8 | convolution fusion | flops 302383104 | bytes 4915200 | tf_op jit(solution)/shard_map/dot_general | solution.py:61
  49.3 3.1 %fusion.115 = (f32[1536]{0:T(1024)S(1)}, f32[128]{0:T(128)S(1)}, f32[1,128,1536]{2,1,0:T(8,128)S(1)}) fusion(bf16[1,128,1536]{2,1,0:T(8,128)(2,1)S(1)} %copy-done, f32[128]{0:T(128)S(1)} %add_rsqrt_fusion, f32[1536]{0:T(1024)S(1)} %copy-done.5, bf16[128,1536]{1,0:T(8,128)(2,1)S(1)} %reverse.7, f32[128,1536]{1,0:T(8,128)S(1)} %fusion.9, ...), kind=kOutput, calls=%fused_computation.99 | convolution fusion | flops 308083072 | bytes 5714944 | tf_op jit(solution)/shard_map/dot_general | solution.py:61
  52.4 1.3 fusion.114
  53.7 5.5 %collective-permute-start = (bf16[1,128,1536]{2,1,0:T(8,128)(2,1)S(1)}, bf16[1,128,1536]{2,1,0:T(8,128)(2,1)S(1)}, u32[]{:S(2)}, u32[]{:S(2)}) collective-permute-start(bf16[1,128,1536]{2,1,0:T(8,128)(2,1)S(1)} %get-tuple-element.6), channel_id=1, source_target_pairs={{0,4},{1,5},{2,6},{3,7},{4,8},{5,9},{6,10},{7,11},{8,12},{9,13},{1... | collective-permute-start | bytes 1179656 | tf_op jit(solution)/shard_map/ppermute | solution.py:14
  59.2 3.6 %collective-permute-start.1 = (bf16[1,128,1536]{2,1,0:T(8,128)(2,1)S(1)}, bf16[1,128,1536]{2,1,0:T(8,128)(2,1)S(1)}, u32[]{:S(2)}, u32[]{:S(2)}) collective-permute-start(bf16[1,128,1536]{2,1,0:T(8,128)(2,1)S(1)} %get-tuple-element.6), channel_id=1, source_target_pairs={{0,2},{1,3},{2,4},{3,5},{4,6},{5,7},{6,8},{7,9},{8,10},{9,11},{10,... | collective-permute-start | bytes 1179656 | tf_op jit(solution)/shard_map/ppermute | solution.py:14
  62.8 1.3 collective-permute-start.2
  64.1 1.3 collective-permute-start.3
  65.4 1.2 rev.34
  66.6 2.1 %fusion.27 = f32[128,768]{1,0:T(8,128)S(1)} fusion(bf16[5,1536,768]{2,1,0:T(8,128)(2,1)} %param.6, bf16[1,128,1536]{2,1,0:T(8,128)(2,1)S(1)} %get-tuple-element.6), kind=kOutput, calls=%fused_computation.31 | convolution fusion | flops 301989888 | bytes 3145728 | tf_op jit(solution)/shard_map/dot_general | solution.py:51
  68.8 5.0 %psum.14 = f32[1536]{0:T(1024)S(1)} all-reduce(f32[1536]{0:T(1024)S(1)} %get-tuple-element.3), channel_id=1, replica_groups=mesh['dp'=2,'ctx'=16] {'dp'}, use_global_device_ids=true, to_apply=%region_3.0 | all-reduce | flops 1536 | bytes 12288 | tf_op jit(solution)/shard_map/psum | solution.py:96
  73.8 34.7 %psum.15 = f32[1536]{0:T(1024)S(1)} all-reduce(f32[1536]{0:T(1024)S(1)} %psum.14), channel_id=1, replica_groups=mesh['dp'=2,'ctx'=16] {'ctx'}, use_global_device_ids=true, to_apply=%region_4.0 | all-reduce | flops 1536 | bytes 12288 | tf_op jit(solution)/shard_map/psum | solution.py:96
  108.5 2.1 %fusion.25 = f32[128,768]{1,0:T(8,128)S(1)} fusion(bf16[5,1536,768]{2,1,0:T(8,128)(2,1)} %param.6, bf16[1,128,1536]{2,1,0:T(8,128)(2,1)S(1)} %rev.34), kind=kOutput, calls=%fused_computation.29 | convolution fusion | flops 301989888 | bytes 3145728 | tf_op jit(solution)/shard_map/dot_general | solution.py:51
  110.7 0.6 broadcast_multiply_fusion
  111.3 1.2 rev.36
  112.5 2.1 %fusion.11 = f32[128,768]{1,0:T(8,128)S(1)} fusion(bf16[5,1536,768]{2,1,0:T(8,128)(2,1)} %param.6, bf16[1,128,1536]{2,1,0:T(8,128)(2,1)S(1)} %rev.36), kind=kOutput, calls=%fused_computation.15 | convolution fusion | flops 301989888 | bytes 3145728 | tf_op jit(solution)/shard_map/dot_general | solution.py:51
  114.7 1.2 rev.35
  115.9 2.1 %fusion.17 = f32[128,768]{1,0:T(8,128)S(1)} fusion(bf16[5,1536,768]{2,1,0:T(8,128)(2,1)} %param.6, bf16[1,128,1536]{2,1,0:T(8,128)(2,1)S(1)} %rev.35), kind=kOutput, calls=%fused_computation.21 | convolution fusion | flops 301989888 | bytes 3145728 | tf_op jit(solution)/shard_map/dot_general | solution.py:51
  118.1 6.7 %rev.33 = bf16[1,128,1536]{2,1,0:T(8,128)(2,1)} reverse(bf16[1,128,1536]{2,1,0:T(8,128)(2,1)} %collective-permute-done.2), dimensions={2} | reverse | bytes 786432 | tf_op jit(solution)/shard_map/rev | solution.py:22
  124.8 2.3 %fusion.33 = f32[128,768]{1,0:T(8,128)S(1)} fusion(bf16[5,1536,768]{2,1,0:T(8,128)(2,1)} %param.6, bf16[1,128,1536]{2,1,0:T(8,128)(2,1)} %rev.33), kind=kOutput, calls=%fused_computation.37 | convolution fusion | flops 301989888 | bytes 3145728 | tf_op jit(solution)/shard_map/dot_general | solution.py:51
  127.1 5.2 %rev.32 = bf16[1,128,1536]{2,1,0:T(8,128)(2,1)S(1)} reverse(bf16[1,128,1536]{2,1,0:T(8,128)(2,1)} %collective-permute-done.3), dimensions={2} | reverse | bytes 786432 | tf_op jit(solution)/shard_map/rev | solution.py:22
  132.3 2.2 %fusion.90 = bf16[128,768]{1,0:T(8,128)(2,1)S(1)} fusion(f32[128,768]{1,0:T(8,128)S(1)} %fusion.11, f32[128,768]{1,0:T(8,128)S(1)} %fusion.17, f32[128,768]{1,0:T(8,128)S(1)} %fusion.25, f32[128,768]{1,0:T(8,128)S(1)} %fusion.33, bf16[5,1536,768]{2,1,0:T(8,128)(2,1)} %param.6, bf16[1,128,1536]{2,1,0:T(8,128)(2,1)S(1)} %rev.32), kind=kOutput, calls=%fused_computation.76 | convolution fusion | flops 302481408 | bytes 4521984 | tf_op jit(solution)/shard_map/dot_general | solution.py:51
  134.4 0.6 reverse.6
  135.1 2.3 %fusion.13 = f32[128,768]{1,0:T(8,128)S(1)} fusion(bf16[5,1536,768]{2,1,0:T(8,128)(2,1)} %param.6, bf16[1,128,1536]{2,1,0:T(8,128)(2,1)} %collective-permute-done.3), kind=kOutput, calls=%fused_computation.17 | convolution fusion | flops 301989888 | bytes 3145728 | tf_op jit(solution)/shard_map/dot_general | solution.py:51
  137.4 2.3 %fusion.19 = f32[128,768]{1,0:T(8,128)S(1)} fusion(bf16[5,1536,768]{2,1,0:T(8,128)(2,1)} %param.6, bf16[1,128,1536]{2,1,0:T(8,128)(2,1)} %collective-permute-done.2), kind=kOutput, calls=%fused_computation.23 | convolution fusion | flops 301989888 | bytes 3145728 | tf_op jit(solution)/shard_map/dot_general | solution.py:51
  139.7 2.1 %fusion.35 = f32[128,768]{1,0:T(8,128)S(1)} fusion(bf16[5,1536,768]{2,1,0:T(8,128)(2,1)} %param.6, bf16[1,128,1536]{2,1,0:T(8,128)(2,1)S(1)} %collective-permute-done.1), kind=kOutput, calls=%fused_computation.39 | convolution fusion | flops 301989888 | bytes 3145728 | tf_op jit(solution)/shard_map/dot_general | solution.py:51
  141.8 2.9 %fusion.96 = bf16[1,128,768]{2,1,0:T(8,128)(2,1)} fusion(f32[128,768]{1,0:T(8,128)S(1)} %fusion.13, f32[128,768]{1,0:T(8,128)S(1)} %fusion.19, f32[128,768]{1,0:T(8,128)S(1)} %fusion.27, f32[128,768]{1,0:T(8,128)S(1)} %fusion.35, bf16[5,1536,768]{2,1,0:T(8,128)(2,1)} %param.6, bf16[1,128,1536]{2,1,0:T(8,128)(2,1)S(1)} %collective-permute-done, ...), kind=kOutput, calls=%fused_computation.78 | convolution fusion | flops 302678016 | bytes 4718592 | tf_op jit(solution)/shard_map/dot_general | solution.py:51
  (19 shorter events, 0.1 us)
Async XLA Ops:
  0.6 20.1 %collective-permute-start.6 = (bf16[1,128,768]{2,1,0:T(8,128)(2,1)}, bf16[1,128,768]{2,1,0:T(8,128)(2,1)S(1)}, u32[]{:S(2)}, u32[]{:S(2)}) collective-permute-start(bf16[1,128,768]{2,1,0:T(8,128)(2,1)} %param.7), channel_id=1, source_target_pairs={{0,2},{1,3},{2,4},{3,5},{4,6},{5,7},{6,8},{7,9},{8,10},{9,11},{10,... | collective-permute-start | bytes 589832 | tf_op jit(solution)/shard_map/ppermute | solution.py:14
  5.5 18.4 %collective-permute-start.7 = (bf16[1,128,768]{2,1,0:T(8,128)(2,1)}, bf16[1,128,768]{2,1,0:T(8,128)(2,1)S(1)}, u32[]{:S(2)}, u32[]{:S(2)}) collective-permute-start(bf16[1,128,768]{2,1,0:T(8,128)(2,1)} %param.7), channel_id=1, source_target_pairs={{0,4},{1,5},{2,6},{3,7},{4,8},{5,9},{6,10},{7,11},{8,12},{9,13},{1... | collective-permute-start | bytes 589832 | tf_op jit(solution)/shard_map/ppermute | solution.py:14
  9.0 20.5 %collective-permute-start.4 = (bf16[1,128,768]{2,1,0:T(8,128)(2,1)}, bf16[1,128,768]{2,1,0:T(8,128)(2,1)}, u32[]{:S(2)}, u32[]{:S(2)}) collective-permute-start(bf16[1,128,768]{2,1,0:T(8,128)(2,1)} %param.7), channel_id=1, source_target_pairs={{4,0},{5,1},{6,2},{7,3},{8,4},{9,5},{10,6},{11,7},{12,8},{13,9},{1... | collective-permute-start | bytes 589832 | tf_op jit(solution)/shard_map/ppermute | solution.py:14
  10.3 24.5 %collective-permute-start.5 = (bf16[1,128,768]{2,1,0:T(8,128)(2,1)}, bf16[1,128,768]{2,1,0:T(8,128)(2,1)}, u32[]{:S(2)}, u32[]{:S(2)}) collective-permute-start(bf16[1,128,768]{2,1,0:T(8,128)(2,1)} %param.7), channel_id=1, source_target_pairs={{2,0},{3,1},{4,2},{5,3},{6,4},{7,5},{8,6},{9,7},{10,8},{11,9},{12,... | collective-permute-start | bytes 589832 | tf_op jit(solution)/shard_map/ppermute | solution.py:14
  20.7 3.2 %copy-start.3 = (bf16[1,128,768]{2,1,0:T(8,128)(2,1)}, bf16[1,128,768]{2,1,0:T(8,128)(2,1)S(1)}, u32[]{:S(2)}) copy-start(bf16[1,128,768]{2,1,0:T(8,128)(2,1)S(1)} %collective-permute-done.6) | copy-start | bytes 589828
  23.9 0.7 copy-start.1
  26.8 22.4 %copy-start = (bf16[1,128,1536]{2,1,0:T(8,128)(2,1)S(1)}, bf16[1,128,1536]{2,1,0:T(8,128)(2,1)}, u32[]{:S(2)}) copy-start(bf16[1,128,1536]{2,1,0:T(8,128)(2,1)} %param.4) | copy-start | bytes 1179652
  26.8 22.4 %copy-start.5 = (f32[1536]{0:T(1024)S(1)}, f32[1536]{0:T(1024)}, u32[]{:S(2)}) copy-start(f32[1536]{0:T(1024)} %param.5) | copy-start | bytes 18436
  29.6 14.4 %copy-start.2 = (bf16[1,128,768]{2,1,0:T(8,128)(2,1)S(1)}, bf16[1,128,768]{2,1,0:T(8,128)(2,1)}, u32[]{:S(2)}) copy-start(bf16[1,128,768]{2,1,0:T(8,128)(2,1)} %copy-done.1) | copy-start | bytes 589828
  40.1 9.2 %copy-start.4 = (bf16[1,128,768]{2,1,0:T(8,128)(2,1)S(1)}, bf16[1,128,768]{2,1,0:T(8,128)(2,1)}, u32[]{:S(2)}) copy-start(bf16[1,128,768]{2,1,0:T(8,128)(2,1)} %copy-done.3) | copy-start | bytes 589828
  53.7 57.6 %collective-permute-start = (bf16[1,128,1536]{2,1,0:T(8,128)(2,1)S(1)}, bf16[1,128,1536]{2,1,0:T(8,128)(2,1)S(1)}, u32[]{:S(2)}, u32[]{:S(2)}) collective-permute-start(bf16[1,128,1536]{2,1,0:T(8,128)(2,1)S(1)} %get-tuple-element.6), channel_id=1, source_target_pairs={{0,4},{1,5},{2,6},{3,7},{4,8},{5,9},{6,10},{7,11},{8,12},{9,13},{1... | collective-permute-start | bytes 1179656 | tf_op jit(solution)/shard_map/ppermute | solution.py:14
  59.2 55.5 %collective-permute-start.1 = (bf16[1,128,1536]{2,1,0:T(8,128)(2,1)S(1)}, bf16[1,128,1536]{2,1,0:T(8,128)(2,1)S(1)}, u32[]{:S(2)}, u32[]{:S(2)}) collective-permute-start(bf16[1,128,1536]{2,1,0:T(8,128)(2,1)S(1)} %get-tuple-element.6), channel_id=1, source_target_pairs={{0,2},{1,3},{2,4},{3,5},{4,6},{5,7},{6,8},{7,9},{8,10},{9,11},{10,... | collective-permute-start | bytes 1179656 | tf_op jit(solution)/shard_map/ppermute | solution.py:14
  62.8 55.2 %collective-permute-start.2 = (bf16[1,128,1536]{2,1,0:T(8,128)(2,1)S(1)}, bf16[1,128,1536]{2,1,0:T(8,128)(2,1)}, u32[]{:S(2)}, u32[]{:S(2)}) collective-permute-start(bf16[1,128,1536]{2,1,0:T(8,128)(2,1)S(1)} %get-tuple-element.6), channel_id=1, source_target_pairs={{2,0},{3,1},{4,2},{5,3},{6,4},{7,5},{8,6},{9,7},{10,8},{11,9},{12,... | collective-permute-start | bytes 1179656 | tf_op jit(solution)/shard_map/ppermute | solution.py:14
  64.1 62.9 %collective-permute-start.3 = (bf16[1,128,1536]{2,1,0:T(8,128)(2,1)S(1)}, bf16[1,128,1536]{2,1,0:T(8,128)(2,1)}, u32[]{:S(2)}, u32[]{:S(2)}) collective-permute-start(bf16[1,128,1536]{2,1,0:T(8,128)(2,1)S(1)} %get-tuple-element.6), channel_id=1, source_target_pairs={{4,0},{5,1},{6,2},{7,3},{8,4},{9,5},{10,6},{11,7},{12,8},{13,9},{1... | collective-permute-start | bytes 1179656 | tf_op jit(solution)/shard_map/ppermute | solution.py:14
